TPU v7x, 128 devices: a whole 4x4x4 slice. The times are simulated.
128 devices in a mesh: context: 8 (over z, core), tensor: 16 (over x, y).
Axes of the slice: x: 4, y: 4, z: 4, core: 2. Of those that a mesh axis runs over, the one named last changes fastest.
Arguments:
- features: bfloat16 [4096, 3, 8192], P('context', None, 'tensor'), may hold values from -6 to 6
- se_filter: float32 [7, 3, 8192], P(None, None, 'tensor'), may hold values from -1.6 to 1.6
- mr_filter: bfloat16 [128, 512], P(None, 'tensor'), may hold values from -0.61 to 0.61
- stream: bfloat16 [4096, 8192], P('context', 'tensor'), may hold values from -20 to 20
- w_out: bfloat16 [8192, 8192], P('tensor'), may hold values from -0.09375 to 0.09375
- norm_gain: float32 [8192], replicated, may hold values from 0.1 to 1.9
- w_qkv: bfloat16 [8192, 3, 4096], P(None, None, 'tensor'), as said below
Outputs:
- stream_out: bfloat16 [4096, 8192], P('context', 'tensor')
- context_out: bfloat16 [4096, 4096], P('context', 'tensor')
Inputs may be any that keep to these rules, and one draw needn't show every extreme that they name: `w_qkv`: projection weights.
All inputs are finite; a program needn't handle non-finite values.
Results may differ from a plain program's by a relative error of at most 0.019.
Values may be sent and summed in bfloat16 or wider, within the bound.
No kernel may reach another device: no remote copies, remote signals or barrier semaphores. Data moves between devices by JAX's collectives and lax.ppermute only.
A program may use at most 192 MiB of HBM per device.

v0:
```python
import jax
import jax.numpy as jnp
from jax import lax
from jax.sharding import PartitionSpec as P

HD = 128


def passed_along(value, axis, steps):
    count = lax.axis_size(axis)
    initial, last = (max(0, -steps), min(count, count - steps))
    return lax.ppermute(value, axis, [(source, source + steps) for source in range(initial, last)])


def short_filter(padded, se_filter, row_count):
    se_width = se_filter.shape[0]
    filtered = se_filter[0][None] * padded[se_width - 1 : se_width - 1 + row_count].astype(
        jnp.float32
    )
    for offset_lag in range(1, se_width):
        window = padded[se_width - 1 - offset_lag : se_width - 1 - offset_lag + row_count].astype(
            jnp.float32
        )
        filtered = filtered + se_filter[offset_lag][None] * window
    return filtered


def toeplitz_blocks(mr_filter):
    blocks = mr_filter.shape[0]
    groups = mr_filter.shape[1]
    reversed_taps = mr_filter[::-1].T
    period_row = jnp.concatenate([reversed_taps, jnp.zeros((groups, blocks), jnp.bfloat16)], axis=1)
    tiled = jnp.tile(period_row, (1, blocks))[:, : blocks * (2 * blocks - 1)]
    tiled = tiled.reshape(groups, blocks, 2 * blocks - 1)
    return jnp.concatenate([tiled, jnp.zeros((groups, blocks, 1), jnp.bfloat16)], axis=2)


def medium_filter(kv_prev, kv_prod, mr_filter):
    tok_rows, own_chans = kv_prod.shape
    blocks = mr_filter.shape[0]
    groups = mr_filter.shape[1]
    group_width = own_chans // groups
    block_count = tok_rows // blocks
    extended = jnp.concatenate([kv_prev, kv_prod, jnp.zeros((1, own_chans), jnp.bfloat16)], axis=0)
    lower = extended[:tok_rows].reshape(block_count, blocks, groups, group_width)
    upper = extended[blocks : blocks + tok_rows].reshape(block_count, blocks, groups, group_width)
    toeplitz = toeplitz_blocks(mr_filter)
    medium = jnp.einsum(
        "gim,bmgc->bigc", toeplitz[:, :, :blocks], lower, preferred_element_type=jnp.float32
    )
    medium = medium + jnp.einsum(
        "gim,bmgc->bigc", toeplitz[:, :, blocks:], upper, preferred_element_type=jnp.float32
    )
    return medium.reshape(tok_rows, own_chans)


def on_device(features, se_filter, mr_filter, stream, w_out, norm_gain, w_qkv):
    tok_rows = features.shape[0]
    own_chans = features.shape[2]
    se_width = se_filter.shape[0]
    mr_width = mr_filter.shape[0]
    edge_rows = passed_along(features[tok_rows - (se_width - 1) :], "context", 1)
    short_out = short_filter(jnp.concatenate([edge_rows, features], axis=0), se_filter, tok_rows)
    kv_prod = (short_out[:, 1, :] * short_out[:, 2, :]).astype(jnp.bfloat16)
    kv_prev = passed_along(kv_prod[tok_rows - (mr_width - 1) :], "context", 1)
    medium = medium_filter(kv_prev, kv_prod, mr_filter)
    gated = (short_out[:, 0, :] * medium).astype(jnp.bfloat16)
    tensor_rank = lax.axis_index("tensor")
    partial_value = jnp.dot(gated, w_out, preferred_element_type=jnp.float32)
    own_cols = lax.dynamic_slice_in_dim(
        partial_value, tensor_rank * own_chans, own_chans, 1
    ) + stream.astype(jnp.float32)
    term_all = lax.dynamic_update_slice_in_dim(partial_value, own_cols, tensor_rank * own_chans, 1)
    mixed_rows = lax.psum(term_all, "tensor")
    stream_out = lax.dynamic_slice_in_dim(mixed_rows, tensor_rank * own_chans, own_chans, 1).astype(
        jnp.bfloat16
    )
    mean_square = jnp.mean(mixed_rows * mixed_rows, axis=1, keepdims=True)
    normed = (mixed_rows * lax.rsqrt(mean_square + 1e-05) * norm_gain[None, :]).astype(jnp.bfloat16)
    qkv_proj = jnp.einsum("td,dkh->tkh", normed, w_qkv, preferred_element_type=jnp.float32).astype(
        jnp.bfloat16
    )
    head_cols = w_qkv.shape[2]
    head_count = head_cols // HD
    query = qkv_proj[:, 0, :].reshape(tok_rows, head_count, HD)
    position = lax.axis_index("context") * tok_rows + jnp.arange(tok_rows, dtype=jnp.int32)
    scale_factor = HD ** (-0.5)
    run_max = jnp.full((head_count, tok_rows), -1e30, jnp.float32)
    key_block = lax.all_gather(qkv_proj[:, 1, :], "context", axis=0, tiled=True)
    value_block = lax.all_gather(qkv_proj[:, 2, :], "context", axis=0, tiled=True)
    key_count = key_block.shape[0]
    keys_three = key_block.reshape(key_count, head_count, HD)
    values_three = value_block.reshape(key_count, head_count, HD)
    scores = (
        jnp.einsum("qhd,khd->hqk", query, keys_three, preferred_element_type=jnp.float32)
        * scale_factor
    )
    key_position = jnp.arange(key_count, dtype=jnp.int32)
    allowed = key_position[None, :] <= position[:, None]
    scores = jnp.where(allowed[None], scores, -jnp.inf)
    new_max = jnp.maximum(run_max, jnp.max(scores, axis=2))
    expo = jnp.exp(scores - new_max[:, :, None])
    run_total = jnp.sum(expo, axis=2)
    weights = expo.astype(jnp.bfloat16)
    run_acc = jnp.einsum("hqk,khd->hqd", weights, values_three, preferred_element_type=jnp.float32)
    run_max, run_total, run_acc = (new_max, run_total, run_acc)
    result = run_acc / run_total[:, :, None]
    context_out = jnp.transpose(result, (1, 0, 2)).reshape(tok_rows, head_cols).astype(jnp.bfloat16)
    return (stream_out, context_out)


def solution(mesh):
    placed = (
        P("context", None, "tensor"),
        P(None, None, "tensor"),
        P(None, "tensor"),
        P("context", "tensor"),
        P("tensor", None),
        P(),
        P(None, None, "tensor"),
    )
    return jax.shard_map(
        on_device,
        mesh=mesh,
        in_specs=placed,
        out_specs=(P("context", "tensor"), P("context", "tensor")),
        check_vma=False,
    )
```

profile of v0, /device:TPU:1, one launch (start us, length us, event | category | flops | bytes accessed | tf_op | source)
XLA Modules:
  0.0 383.0 jit_solution(14725790758552800340)
XLA Ops:
  7.2 0.0 copy-start.4
  7.2 0.0 all-reduce.5.cloned.1.call-start
  7.2 0.7 slice.85
  8.0 0.3 copy.14
  8.2 4.9 %collective-permute-start = (bf16[6,3,512]{0,2,1:T(8,128)(2,1)S(1)}, bf16[6,3,512]{0,2,1:T(8,128)(2,1)S(1)}, u32[]{:S(2)}, u32[]{:S(2)}) collective-permute-start(bf16[6,3,512]{0,2,1:T(8,128)(2,1)S(1)} %copy.14), channel_id=1, source_target_pairs={{0,16},{16,32},{32,48},{48,64},{64,80},{80,96},{96,112},{1,17},{17... | collective-permute-start | bytes 55304 | tf_op jit(solution)/shard_map/ppermute | solution.py:12
  13.2 1.2 fusion.42
  14.4 0.6 copy_bitcast_fusion.2
  15.0 0.6 copy_bitcast_fusion.4
  15.6 2.6 copy.13
  18.2 0.0 copy-done.4
  18.2 0.1 rev.3
  18.3 0.1 tile.4
  18.5 1.2 copy.35
  19.7 0.1 slice.124
  19.8 7.8 %reshape.68 = bf16[32,128,255]{2,1,0:T(8,128)(2,1)} reshape(bf16[32,32640]{1,0:T(8,128)(2,1)S(1)} %slice.124) | data formatting | bytes 4177920 | tf_op jit(solution)/shard_map/reshape | solution.py:34
  27.6 0.6 copy.50
  28.2 0.0 collective-permute-done
  28.2 12.6 %multiply_add_fusion = f32[512,3,512]{0,2,1:T(8,128)S(1)} fusion(bf16[512,3,512]{0,2,1:T(8,128)(2,1)} %copy.13, bf16[6,3,512]{0,2,1:T(8,128)(2,1)S(1)} %collective-permute-done, f32[3,512]{1,0:T(4,128)S(1)} %get-tuple-element.20, f32[3,512]{1,0:T(4,128)S(1)} %get-tuple-element.21, f32[3,512]{1,0:T(4,128)} %get-tuple-element.22, ...), kind=kLoop, calls=%fused_computation.19 | loop fusion | flops 29884416 | bytes 4780032 | tf_op jit(solution)/shard_map/add | solution.py:24
  40.8 0.2 fusion.27
  41.0 0.1 slice_bitcast_fusion.3
  41.1 1.9 collective-permute-start.1
  43.0 0.2 fusion.48
  43.2 1.8 collective-permute-done.1
  44.9 1.5 pad_maximum_fusion.1
  46.4 2.0 reshape.69
  48.4 2.0 reshape.67
  50.4 0.0 copy-start.1
  50.4 0.0 copy-start.2
  50.4 2.3 fusion.24
  52.7 0.0 copy-done.1
  52.7 0.0 copy-done.2
  52.7 0.8 fusion.19
  53.5 0.4 copy.18
  54.0 0.0 copy-start.3
  54.0 11.6 %fusion.34 = f32[512,8192]{1,0:T(8,128)} fusion(bf16[512,8192]{1,0:T(8,128)(2,1)} %param.11, f32[64,8,4,128]{3,2,1,0:T(4,128)S(1)} %bitcast.73, f32[512,3,512]{0,2,1:T(8,128)S(1)} %multiply_add_fusion), kind=kOutput, calls=%fused_computation.49 | convolution fusion | flops 4295491584 | bytes 27262976 | tf_op jit(solution)/shard_map/dot_general | solution.py:69
  65.6 0.0 copy-done.3
  65.6 2.4 add_dynamic-update-slice_fusion
  68.0 0.0 all-reduce.5.cloned.1.call-update
  68.0 0.0 copy-start.5
  68.0 0.2 all-gather.5.cloned.1.call-start
  68.2 222.7 %all-reduce.5.cloned.1.call-done = f32[512,8192]{1,0:T(8,128)} async-done(((f32[512,8192]{1,0:T(8,128)}), f32[512,8192]{1,0:T(8,128)}) %all-reduce.5.cloned.1.call-update) | async-done | bytes 16777232 | tf_op jit(solution)/shard_map/psum | solution.py:74
  290.9 7.0 %multiply_reduce_fusion = f32[512]{0:T(512)S(1)} fusion(f32[512,8192]{1,0:T(8,128)} %all-reduce.5.cloned.1.call-done), kind=kLoop, calls=%fused_computation.3 | loop fusion | flops 8388096 | bytes 16779264 | tf_op jit(solution)/shard_map/reduce_sum | solution.py:78
  297.9 0.0 copy-done.5
  297.9 14.8 %fusion.16 = bf16[512,3,256]{0,2,1:T(8,128)(2,1)S(1)} fusion(bf16[8192,3,256]{2,0,1:T(8,128)(2,1)} %param.13, f32[512,8192]{1,0:T(8,128)} %all-reduce.5.cloned.1.call-done, f32[8192]{0:T(1024)S(1)} %copy-done.5, f32[512]{0:T(512)S(1)} %add_rsqrt_fusion), kind=kOutput, calls=%fused_computation.32 | convolution fusion | flops 6455427072 | bytes 30181376 | tf_op jit(solution)/shard_map/td,dkh->tkh/dot_general | solution.py:80
  312.7 0.8 fusion.41
  313.5 0.0 all-gather.5.cloned.1.call-update
  313.6 0.0 all-gather.7.cloned.1.call-start
  313.6 0.7 all-gather.7.cloned.1.call-update
  314.3 1.7 iota_compare_fusion
  316.0 2.1 dynamic-slice_convert_fusion
  318.1 21.7 %all-gather.5.cloned.1.call-done = bf16[4096,1,256]{0,2,1:T(8,128)(2,1)} async-done(((bf16[512,1,256]{0,2,1:T(8,128)(2,1)}), bf16[4096,1,256]{0,2,1:T(8,128)(2,1)}) %all-gather.5.cloned.1.call-update) | async-done | bytes 2097168 | tf_op jit(solution)/shard_map/all_gather | solution.py:89
  339.7 5.3 %fusion = (f32[2,512]{1,0:T(2,128)S(1)}, f32[2,512,4096]{2,1,0:T(8,128)S(1)}) fusion(pred[512,4096]{1,0:T(8,128)(4,1)S(1)} %iota_compare_fusion, bf16[512,2,128]{0,2,1:T(8,128)(2,1)S(1)} %bitcast.77, bf16[4096,2,128]{0,2,1:T(8,128)(2,1)} %bitcast.81), kind=kOutput, calls=%fused_computation.4 | convolution fusion | flops 1086323712 | bytes 21237760 | tf_op jit(solution)/shard_map/qhd,khd->hqk/dot_general | solution.py:95
  345.0 0.0 copy-start
  345.1 5.7 %copy-done = f32[2,512,4096]{2,1,0:T(8,128)} copy-done((f32[2,512,4096]{2,1,0:T(8,128)}, f32[2,512,4096]{2,1,0:T(8,128)S(1)}, u32[]{:S(2)}) %copy-start) | copy-done | bytes 16777240
  350.8 4.6 %fusion.1 = f32[2,512]{1,0:T(2,128)S(1)} fusion(f32[2,512,4096]{2,1,0:T(8,128)S(1)} %get-tuple-element.19, f32[2,512]{1,0:T(2,128)S(1)} %broadcast_maximum_fusion, pred[512,4096]{1,0:T(8,128)(4,1)S(1)} %iota_compare_fusion), kind=kLoop, calls=%fused_computation.5 | loop fusion | flops 16776192 | bytes 18882560 | tf_op jit(solution)/shard_map/reduce_sum | solution.py:103
  355.4 11.9 %all-gather.7.cloned.1.call-done = bf16[4096,1,256]{0,2,1:T(8,128)(2,1)} async-done(((bf16[512,1,256]{0,2,1:T(8,128)(2,1)}), bf16[4096,1,256]{0,2,1:T(8,128)(2,1)}) %all-gather.7.cloned.1.call-update) | async-done | bytes 2097168 | tf_op jit(solution)/shard_map/all_gather | solution.py:90
  367.2 8.4 %fusion.31 = bf16[512,2,128]{0,2,1:T(8,128)(2,1)S(1)} fusion(bf16[4096,2,128]{0,2,1:T(8,128)(2,1)} %bitcast.82, f32[2,512,4096]{2,1,0:T(8,128)} %copy-done, f32[2,512]{1,0:T(2,128)S(1)} %broadcast_maximum_fusion, pred[512,4096]{1,0:T(8,128)(4,1)S(1)} %iota_compare_fusion, f32[512,2]{0,1:T(2,128)S(1)} %bitcast.80), kind=kOutput, calls=%fused_computation.47 | convolution fusion | flops 1090781184 | bytes 21241856 | tf_op jit(solution)/shard_map/hqk,khd->hqd/dot_general | solution.py:105
  375.7 0.8 copy.22
  (5 shorter events, 0.0 us)
Async XLA Ops:
  7.2 11.1 %copy-start.4 = (bf16[128,32]{0,1:T(8,128)(2,1)S(1)}, bf16[128,32]{0,1:T(8,128)(2,1)}, u32[]{:S(2)}) copy-start(bf16[128,32]{0,1:T(8,128)(2,1)} %param.9) | copy-start | bytes 24580
  7.2 283.8 %all-reduce.5.cloned.1.call-start = ((), (), s32[]{:S(2)}) async-start(), calls=%async_computation | async-start | bytes 33554432 | tf_op jit(solution)/shard_map/psum | solution.py:74
  8.2 20.0 %collective-permute-start = (bf16[6,3,512]{0,2,1:T(8,128)(2,1)S(1)}, bf16[6,3,512]{0,2,1:T(8,128)(2,1)S(1)}, u32[]{:S(2)}, u32[]{:S(2)}) collective-permute-start(bf16[6,3,512]{0,2,1:T(8,128)(2,1)S(1)} %copy.14), channel_id=1, source_target_pairs={{0,16},{16,32},{32,48},{48,64},{64,80},{80,96},{96,112},{1,17},{17... | collective-permute-start | bytes 55304 | tf_op jit(solution)/shard_map/ppermute | solution.py:12
  41.1 3.9 %collective-permute-start.1 = (bf16[127,512]{0,1:T(8,128)(2,1)S(1)}, bf16[127,512]{0,1:T(8,128)(2,1)S(1)}, u32[]{:S(2)}, u32[]{:S(2)}) collective-permute-start(bf16[127,512]{0,1:T(8,128)(2,1)S(1)} %slice_bitcast_fusion.3), channel_id=1, source_target_pairs={{0,16},{16,32},{32,48},{48,64},{64,80},{80,96},{96,112},{1,17},{17... | collective-permute-start | bytes 390152 | tf_op jit(solution)/shard_map/ppermute | solution.py:12
  50.4 2.3 copy-start.1
  50.4 2.4 copy-start.2
  54.0 11.6 %copy-start.3 = (bf16[512,512]{1,0:T(8,128)(2,1)S(1)}, bf16[512,512]{1,0:T(8,128)(2,1)}, u32[]{:S(2)}) copy-start(bf16[512,512]{1,0:T(8,128)(2,1)} %param.10) | copy-start | bytes 1572868
  68.0 229.9 %copy-start.5 = (f32[8192]{0:T(1024)S(1)}, f32[8192]{0:T(1024)}, u32[]{:S(2)}) copy-start(f32[8192]{0:T(1024)} %param.12) | copy-start | bytes 98308
  68.0 271.8 %all-gather.5.cloned.1.call-start = ((), (), s32[]{:S(2)}) async-start(), calls=%async_computation.1 | async-start | bytes 2359296 | tf_op jit(solution)/shard_map/all_gather | solution.py:89
  313.6 53.7 %all-gather.7.cloned.1.call-start = ((), (), s32[]{:S(2)}) async-start(), calls=%async_computation.2 | async-start | bytes 2359296 | tf_op jit(solution)/shard_map/all_gather | solution.py:90
  345.0 5.7 %copy-start = (f32[2,512,4096]{2,1,0:T(8,128)}, f32[2,512,4096]{2,1,0:T(8,128)S(1)}, u32[]{:S(2)}) copy-start(f32[2,512,4096]{2,1,0:T(8,128)S(1)} %get-tuple-element.19) | copy-start | bytes 50331652
Sparse Core Ops, SparseCore 0:
  68.1 222.7 all-reduce.4
  313.7 26.0 all-gather.4
  341.4 25.7 all-gather.6
where the time goes:
time: 384 us; the launch traced here: 383 us
  waiting for transfers between devices  259 us (67%)
  matrix products  43.2 us (11%)
  local copies, waits for them, and re-layouts  30 us (8%)
  other arithmetic  30 us (8%)
  between operations  13.9 us (4%)
  starting transfers between devices  7.16 us (2%)
    psum x1, waiting for transfers between devices, on_device(): mixed_rows = lax.psum(term_all, 'tensor')  223 us
    all_gather x1, waiting for transfers between devices, on_device(): key_block = lax.all_gather(qkv_proj[:, 1, :], 'context', axis=0, tiled=True)  21.7 us
    dot_general x1, matrix products, on_device(): jnp.einsum('td,dkh->tkh', normed, w_qkv, preferred_element_type=jnp.float32)  14.8 us
    add x1, other arithmetic, short_filter(): filtered = filtered + se_filter[offset_lag][None] * window  12.6 us
    unnamed x19, local copies, waits for them, and re-layouts  12.2 us
    all_gather x1, waiting for transfers between devices, on_device(): lax.all_gather(qkv_proj[:, 2, :], 'context', axis=0, tiled=True)  11.9 us
    dot_general x1, matrix products, on_device(): partial_value = jnp.dot(gated, w_out, preferred_element_type=jnp.float32)  11.6 us
    dot_general x1, matrix products, on_device(): jnp.einsum('hqk,khd->hqd', weights, values_three, preferred_element_type=...  8.42 us
  transfers between devices with their start and end apart: 5, of which 4 were waited for; matrix products, arithmetic and copies ran while one was open for 8% of the time, Pallas kernels for 0%

commit v1 on v0

--- a/solution.py
+++ b/solution.py
@@ -71,7 +71,11 @@
         partial_value, tensor_rank * own_chans, own_chans, 1
     ) + stream.astype(jnp.float32)
     term_all = lax.dynamic_update_slice_in_dim(partial_value, own_cols, tensor_rank * own_chans, 1)
-    mixed_rows = lax.psum(term_all, "tensor")
+    count_all = jax.lax.axis_size("tensor")
+    mixed_rows = term_all
+    for tick in [j0 for j0 in (1, 2, 4, 8, 16) if j0 < count_all]:
+        mat_out = jax.lax.ppermute(mixed_rows, "tensor", [(u, u ^ tick) for u in range(count_all)])
+        mixed_rows = mixed_rows + mat_out
     stream_out = lax.dynamic_slice_in_dim(mixed_rows, tensor_rank * own_chans, own_chans, 1).astype(
         jnp.bfloat16
     )

time: 384 us -> 1640 us (4.27)
  waiting for transfers between devices: 259 us -> 1480 us
  other arithmetic: 30 us -> 67.4 us
    ppermute x0 -> x4, waiting for transfers between devices: none -> 1440 us  [on_device(): jax.lax.ppermute(mixed_rows, 'tensor', [(u, u ^ tick) for u in range(coun...]
    psum x1 -> x0, waiting for transfers between devices: 223 us -> none  [on_device(): mixed_rows = lax.psum(term_all, 'tensor')]
    add x0 -> x3, other arithmetic: none -> 34.8 us  [on_device(): mixed_rows = mixed_rows + mat_out]
  transfers between devices with their start and end apart: 5 -> 8, of which waited for: 4 -> 7; matrix products, arithmetic and copies ran while one was open for 8% -> 2% of each run, Pallas kernels for 0% -> 0%
where the time goes in v1:
time: 1640 us
  waiting for transfers between devices  1480 us (90%)
  other arithmetic  67.4 us (4%)
  matrix products  38.8 us (2%)
  local copies, waits for them, and re-layouts  30 us (2%)
    ppermute x4, waiting for transfers between devices, on_device(): jax.lax.ppermute(mixed_rows, 'tensor', [(u, u ^ tick) for u in range(coun...  1440 us
    add x3, other arithmetic, on_device(): mixed_rows = mixed_rows + mat_out  34.8 us
  transfers between devices with their start and end apart: 8, of which 7 were waited for; matrix products, arithmetic and copies ran while one was open for 2% of the time, Pallas kernels for 0%

profile of v1, /device:TPU:1, one launch (start us, length us, event | category | flops | bytes accessed | tf_op | source)
XLA Modules:
  0.0 1642.0 jit_solution(11948876182535776036)
XLA Ops:
  7.2 0.0 copy-start.4
  7.2 0.0 all-gather.5.cloned.1.call-start
  7.2 0.7 slice.85
  8.0 0.3 copy.14
  8.2 4.9 collective-permute-start
  13.2 1.2 fusion.42
  14.4 0.6 copy_bitcast_fusion.2
  15.0 0.6 copy_bitcast_fusion.4
  15.6 2.6 copy.13
  18.2 0.6 copy.50
  18.8 0.0 copy-done.4
  18.8 0.1 rev.3
  18.9 0.1 tile.4
  19.0 1.2 copy.35
  20.2 0.1 slice.124
  20.4 7.8 reshape.68
  28.2 0.0 collective-permute-done
  28.2 12.4 multiply_add_fusion
  40.5 0.2 fusion.27
  40.7 0.1 slice_bitcast_fusion.3
  40.8 1.9 collective-permute-start.1
  42.7 0.2 fusion.48
  42.9 1.8 collective-permute-done.1
  44.7 1.5 pad_maximum_fusion.1
  46.1 2.0 reshape.69
  48.1 2.0 reshape.67
  50.1 0.0 copy-start.1
  50.1 2.3 fusion.24
  52.4 0.0 copy-done.1
  52.4 0.0 copy-done.2
  52.4 0.8 fusion.19
  53.3 0.4 copy.18
  53.7 0.0 copy-start.3
  53.7 7.2 fusion.34
  60.9 0.0 copy-done.3
  60.9 0.2 add_dynamic-update-slice_fusion
  61.1 1.4 collective-permute-start.2
  62.5 361.0 %collective-permute-done.2 = f32[512,8192]{1,0:T(8,128)} collective-permute-done((f32[512,8192]{1,0:T(8,128)S(1)}, f32[512,8192]{1,0:T(8,128)}, u32[]{:S(2)}, u32[]{:S(2)}) %collective-permute-start.2) | collective-permute-done | bytes 16777248 | tf_op jit(solution)/shard_map/ppermute | solution.py:77
  423.6 11.7 add.81
  435.3 2.9 collective-permute-start.3
  438.2 360.3 %collective-permute-done.3 = f32[512,8192]{1,0:T(8,128)} collective-permute-done((f32[512,8192]{1,0:T(8,128)}, f32[512,8192]{1,0:T(8,128)}, u32[]{:S(2)}, u32[]{:S(2)}) %collective-permute-start.3) | collective-permute-done | bytes 16777248 | tf_op jit(solution)/shard_map/ppermute | solution.py:77
  798.5 11.3 add.82
  809.8 1.3 collective-permute-start.4
  811.1 359.4 %collective-permute-done.4 = f32[512,8192]{1,0:T(8,128)} collective-permute-done((f32[512,8192]{1,0:T(8,128)S(1)}, f32[512,8192]{1,0:T(8,128)}, u32[]{:S(2)}, u32[]{:S(2)}) %collective-permute-start.4) | collective-permute-done | bytes 16777248 | tf_op jit(solution)/shard_map/ppermute | solution.py:77
  1170.5 11.8 add.83
  1182.3 2.7 collective-permute-start.5
  1185.0 358.5 %collective-permute-done.5 = f32[512,8192]{1,0:T(8,128)S(1)} collective-permute-done((f32[512,8192]{1,0:T(8,128)}, f32[512,8192]{1,0:T(8,128)S(1)}, u32[]{:S(2)}, u32[]{:S(2)}) %collective-permute-start.5) | collective-permute-done | bytes 16777248 | tf_op jit(solution)/shard_map/ppermute | solution.py:77
  1543.5 12.0 multiply_reduce_fusion
  1555.5 0.0 copy-done.5
  1555.5 14.8 fusion.16
  1570.3 0.8 fusion.41
  1571.2 0.0 all-gather.5.cloned.1.call-update
  1571.2 0.3 all-gather.7.cloned.1.call-start
  1571.5 0.5 all-gather.7.cloned.1.call-update
  1572.0 1.7 iota_compare_fusion
  1573.6 2.1 dynamic-slice_convert_fusion
  1575.7 22.7 %all-gather.5.cloned.1.call-done = bf16[4096,1,256]{0,2,1:T(8,128)(2,1)} async-done(((bf16[512,1,256]{0,2,1:T(8,128)(2,1)}), bf16[4096,1,256]{0,2,1:T(8,128)(2,1)}) %all-gather.5.cloned.1.call-update) | async-done | bytes 2097168 | tf_op jit(solution)/shard_map/all_gather | solution.py:93
  1598.5 5.3 fusion
  1603.7 0.0 copy-start
  1603.8 5.7 copy-done
  1609.5 4.6 fusion.1
  1614.1 11.9 all-gather.7.cloned.1.call-done
  1625.9 8.4 fusion.31
  1634.4 0.8 copy.22
  (7 shorter events, 0.0 us)
Async XLA Ops:
  7.2 11.6 copy-start.4
  7.2 1591.3 %all-gather.5.cloned.1.call-start = ((), (), s32[]{:S(2)}) async-start(), calls=%async_computation | async-start | bytes 2359296 | tf_op jit(solution)/shard_map/all_gather | solution.py:93
  8.2 19.9 %collective-permute-start = (bf16[6,3,512]{0,2,1:T(8,128)(2,1)S(1)}, bf16[6,3,512]{0,2,1:T(8,128)(2,1)S(1)}, u32[]{:S(2)}, u32[]{:S(2)}) collective-permute-start(bf16[6,3,512]{0,2,1:T(8,128)(2,1)S(1)} %copy.14), channel_id=1, source_target_pairs={{0,16},{16,32},{32,48},{48,64},{64,80},{80,96},{96,112},{1,17},{17... | collective-permute-start | bytes 55304 | tf_op jit(solution)/shard_map/ppermute | solution.py:12
  40.8 3.9 collective-permute-start.1
  50.1 2.3 copy-start.1
  50.1 2.4 copy-start.2
  53.7 7.2 copy-start.3
  61.1 362.4 %collective-permute-start.2 = (f32[512,8192]{1,0:T(8,128)S(1)}, f32[512,8192]{1,0:T(8,128)}, u32[]{:S(2)}, u32[]{:S(2)}) collective-permute-start(f32[512,8192]{1,0:T(8,128)S(1)} %add_dynamic-update-slice_fusion), channel_id=1, source_target_pairs={{0,1},{1,0},{2,3},{3,2},{4,5},{5,4},{6,7},{7,6},{8,9},{9,8},{10,11... | collective-permute-start | bytes 50331656 | tf_op jit(solution)/shard_map/ppermute | solution.py:77
  435.3 363.2 %collective-permute-start.3 = (f32[512,8192]{1,0:T(8,128)}, f32[512,8192]{1,0:T(8,128)}, u32[]{:S(2)}, u32[]{:S(2)}) collective-permute-start(f32[512,8192]{1,0:T(8,128)} %add.81), channel_id=1, source_target_pairs={{0,2},{1,3},{2,0},{3,1},{4,6},{5,7},{6,4},{7,5},{8,10},{9,11},{10,... | collective-permute-start | bytes 50331656 | tf_op jit(solution)/shard_map/ppermute | solution.py:77
  809.8 360.7 %collective-permute-start.4 = (f32[512,8192]{1,0:T(8,128)S(1)}, f32[512,8192]{1,0:T(8,128)}, u32[]{:S(2)}, u32[]{:S(2)}) collective-permute-start(f32[512,8192]{1,0:T(8,128)S(1)} %add.82), channel_id=1, source_target_pairs={{0,4},{1,5},{2,6},{3,7},{4,0},{5,1},{6,2},{7,3},{8,12},{9,13},{10,... | collective-permute-start | bytes 50331656 | tf_op jit(solution)/shard_map/ppermute | solution.py:77
  1182.3 373.3 %copy-start.5 = (f32[8192]{0:T(1024)S(1)}, f32[8192]{0:T(1024)}, u32[]{:S(2)}) copy-start(f32[8192]{0:T(1024)} %param.12) | copy-start | bytes 98308
  1182.3 361.3 %collective-permute-start.5 = (f32[512,8192]{1,0:T(8,128)}, f32[512,8192]{1,0:T(8,128)S(1)}, u32[]{:S(2)}, u32[]{:S(2)}) collective-permute-start(f32[512,8192]{1,0:T(8,128)} %add.83), channel_id=1, source_target_pairs={{0,8},{1,9},{2,10},{3,11},{4,12},{5,13},{6,14},{7,15},{8,0},{9,1},... | collective-permute-start | bytes 50331656 | tf_op jit(solution)/shard_map/ppermute | solution.py:77
  1571.2 54.8 %all-gather.7.cloned.1.call-start = ((), (), s32[]{:S(2)}) async-start(), calls=%async_computation.1 | async-start | bytes 2359296 | tf_op jit(solution)/shard_map/all_gather | solution.py:94
  1603.7 5.7 copy-start
Sparse Core Ops, SparseCore 0:
  1571.3 27.1 all-gather.4
  1600.1 25.7 all-gather.6
